TPU v7x, 256 devices: a whole 4x4x8 slice. The times are simulated.
256 devices in a mesh: row: 16 (over x_lo, y, core), col: 16 (over z, x_hi).
Axes of the slice: x: 4 (x_hi: 2, x_lo: 2; x = x_hi * 2 + x_lo), y: 4, z: 8, core: 2. Of those that a mesh axis runs over, the one named last changes fastest.
Arguments:
- block_vecs: float32 [16, 131072], P(None, ('col', 'row')), may hold values from -130 to 130
- direction: float32 [16, 131072], P(None, ('col', 'row')), may hold values from -130 to 130
- blocks: bfloat16 [1024, 32, 128, 128], P('col', 'row'), may hold values from 0 to 4
- block_cols: int32 [1024, 32], P('col', 'row'), may hold values from 0 to 1023, as said below
- live_counts: int32 [1024, 16], P('col', 'row'), may hold values from 1 to 2, as said below
Outputs:
- x_next: float32 [16, 131072], P(None, ('col', 'row'))
- reduced: float32 [48, 48], replicated
- residual: float32 [16, 131072], P(None, ('col', 'row'))
Inputs may be any that keep to these rules, and one draw needn't show every extreme that they name: `block_cols`: A block column index g in slots 2 * r to 2 * r + 1 of any block row satisfies (g // 4) mod 16 == r. `live_counts`: every block row has 2 live slots in at least one segment.
All inputs are finite; a program needn't handle non-finite values.
Results may differ from a plain program's by a relative error of at most 0.0003.
Values sent between devices are 32-bit elements; how exact they have to be, the bound alone decides.
A program may use at most 64 MiB of HBM per device.

v0:
```python
import math
import jax
import jax.numpy as jnp
from jax import lax
from jax.sharding import PartitionSpec as P

highest = lax.Precision.HIGHEST


def outer(left, right):
    return jnp.dot(left, right.T, precision=highest, preferred_element_type=jnp.float32)


def cholesky_lower(matrix):
    order_small = matrix.shape[0]
    places = jnp.arange(order_small, dtype=jnp.int32)

    def column_step(step, lower):
        pick = (places == step).astype(jnp.float32)
        row_now = jnp.sum(lower * pick[:, None], axis=0)
        column_now = jnp.sum(matrix * pick[None, :], axis=1)
        pivot = jnp.sum(column_now * pick) - jnp.sum(row_now * row_now)
        pivot_root = jnp.sqrt(pivot)
        below = (column_now - jnp.sum(lower * row_now[None, :], axis=1)) / pivot_root
        values = jnp.where(places > step, below, jnp.where(places == step, pivot_root, 0.0))
        return lower + values[:, None] * pick[None, :]

    return lax.fori_loop(0, order_small, column_step, jnp.zeros_like(matrix))


def solve_lower(lower, right):
    order_small = lower.shape[0]
    places = jnp.arange(order_small, dtype=jnp.int32)

    def row_step(step, solved):
        pick = (places == step).astype(jnp.float32)
        row_now = jnp.sum(lower * pick[:, None], axis=0)
        pivot = jnp.sum(row_now * pick)
        right_row = jnp.sum(right * pick[:, None], axis=0)
        value = (right_row - jnp.sum(row_now[:, None] * solved, axis=0)) / pivot
        return solved + pick[:, None] * value[None, :]

    return lax.fori_loop(0, order_small, row_step, jnp.zeros_like(right))


def solve_upper_t(lower, right):
    order_small = lower.shape[0]
    places = jnp.arange(order_small, dtype=jnp.int32)

    def row_step(count, solved):
        step = order_small - 1 - count
        pick = (places == step).astype(jnp.float32)
        column_now = jnp.sum(lower * pick[None, :], axis=1)
        pivot = jnp.sum(column_now * pick)
        right_row = jnp.sum(right * pick[:, None], axis=0)
        value = (right_row - jnp.sum(column_now[:, None] * solved, axis=0)) / pivot
        return solved + pick[:, None] * value[None, :]

    return lax.fori_loop(0, order_small, row_step, jnp.zeros_like(right))


def local_layout(block_cols, live_counts, span_rows, block_size, row_count):
    per_span = span_rows // block_size
    span_index = block_cols // per_span
    local_cols = span_index // row_count * per_span + block_cols % per_span
    slot_count = block_cols.shape[1]
    live_mask = (jnp.arange(slot_count, dtype=jnp.int32)[None, :] < live_counts).astype(jnp.float32)
    return (local_cols, live_mask)


def forward_part(col_panel, blocks, local_cols, live_mask):
    vec_width = col_panel.shape[0]
    block_size = blocks.shape[2]
    col_blocks = col_panel.reshape(vec_width, -1, block_size)
    picked = col_blocks[:, local_cols, :] * live_mask[None, :, :, None]
    forward = jnp.einsum(
        "vbkj,bkij->vbi", picked, blocks, precision=highest, preferred_element_type=jnp.float32
    )
    return 0.5 * forward.reshape(vec_width, -1)


def backward_part(row_panel, col_length, blocks, local_cols, live_mask):
    vec_width = row_panel.shape[0]
    block_size = blocks.shape[2]
    row_blocks = row_panel.reshape(vec_width, -1, block_size)
    backward = (
        jnp.einsum(
            "vbi,bkij->vbkj",
            row_blocks,
            blocks,
            precision=highest,
            preferred_element_type=jnp.float32,
        )
        * live_mask[None, :, :, None]
    )
    spread = jnp.zeros((vec_width, col_length // block_size, block_size), jnp.float32)
    spread = spread.at[:, local_cols.reshape(-1), :].add(
        backward.reshape(vec_width, -1, block_size)
    )
    return 0.5 * spread.reshape(vec_width, -1)


def per_device(block_vecs, direction, blocks, block_cols, live_counts):
    row_count = lax.axis_size("row")
    col_count = lax.axis_size("col")
    vec_width = block_vecs.shape[0]
    span_rows = block_vecs.shape[1]
    order_total = span_rows * row_count * col_count
    col_length = span_rows * col_count
    block_size = blocks.shape[2]
    local_cols, live_mask = local_layout(block_cols, live_counts, span_rows, block_size, row_count)
    paired = jnp.concatenate([block_vecs, direction], axis=0)
    pair_cols = lax.all_gather(paired, "col", axis=1, tiled=True)
    pair_rows = lax.all_gather(paired, "row", axis=1, tiled=True)
    forward = forward_part(pair_cols, blocks, local_cols, live_mask)
    backward = backward_part(pair_rows, col_length, blocks, local_cols, live_mask)
    image_pair = lax.psum_scatter(
        forward, "row", scatter_dimension=1, tiled=True
    ) + lax.psum_scatter(backward, "col", scatter_dimension=1, tiled=True)
    image_x = image_pair[:vec_width]
    image_p = image_pair[vec_width:]
    gram_x, cross_x = lax.psum(
        (outer(block_vecs, block_vecs), outer(block_vecs, image_x)), ("row", "col")
    )
    factor_x = cholesky_lower(gram_x)
    coefficient = solve_upper_t(factor_x, solve_lower(factor_x, cross_x))
    resid = image_x - jnp.dot(
        coefficient.T, block_vecs, precision=highest, preferred_element_type=jnp.float32
    )
    basis = jnp.concatenate([block_vecs, resid, direction], axis=0)
    resid_cols = lax.all_gather(resid, "col", axis=1, tiled=True)
    resid_rows = lax.all_gather(resid, "row", axis=1, tiled=True)
    forward_r = forward_part(resid_cols, blocks, local_cols, live_mask)
    column_x = outer(basis, image_x)
    column_p = outer(basis, image_p)
    backward_r = backward_part(resid_rows, col_length, blocks, local_cols, live_mask)
    image_r = lax.psum_scatter(
        forward_r, "row", scatter_dimension=1, tiled=True
    ) + lax.psum_scatter(backward_r, "col", scatter_dimension=1, tiled=True)
    column_r = outer(basis, image_r)
    gram_apply = jnp.concatenate([column_x, column_r, column_p], axis=1)
    gram_basis, gram_apply = lax.psum((outer(basis, basis), gram_apply), ("row", "col"))
    factor = cholesky_lower(gram_basis)
    halfway = solve_lower(factor, 0.5 * (gram_apply + gram_apply.T))
    reduced = solve_lower(factor, halfway.T)
    shifted = reduced + 3.0 * jnp.eye(3 * vec_width, dtype=jnp.float32)
    target = jnp.dot(
        shifted, shifted[:, :vec_width], precision=highest, preferred_element_type=jnp.float32
    )
    mixing = solve_upper_t(factor, target)
    fresh = jnp.dot(mixing.T, basis, precision=highest, preferred_element_type=jnp.float32)
    gram_fresh = lax.psum(outer(fresh, fresh), ("row", "col"))
    factor_fresh = cholesky_lower(gram_fresh)
    x_next = math.sqrt(order_total) * solve_lower(factor_fresh, fresh)
    return (x_next, reduced, resid)


def solution(mesh):
    return jax.shard_map(
        per_device,
        mesh=mesh,
        in_specs=(
            P(None, ("col", "row")),
            P(None, ("col", "row")),
            P("col", "row", None, None),
            P("col", "row"),
            P("col", "row"),
        ),
        out_specs=(P(None, ("col", "row")), P(), P(None, ("col", "row"))),
        check_vma=False,
    )
```

profile of v0, /device:TPU:1, one launch (start us, length us, event | category | flops | bytes accessed | tf_op | source)
XLA Modules:
  0.0 1421.3 jit_solution(11187509048310806808)
XLA Ops:
  11.9 37.2 %all-gather.5.cloned.1.call-done = f32[32,8192]{1,0:T(8,128)} async-done(((f32[32,512]{1,0:T(8,128)}), f32[32,8192]{1,0:T(8,128)}) %all-gather.5.cloned.1.call-update) | async-done | bytes 1048592 | tf_op jit(solution)/shard_map/all_gather | solution.py:114
  54.9 5.7 scatter_fusion
  62.0 64.4 %all-gather.3.cloned.1.call-done = f32[32,8192]{1,0:T(8,128)} async-done(((f32[32,512]{1,0:T(8,128)}), f32[32,8192]{1,0:T(8,128)}) %all-gather.3.cloned.1.call-update) | async-done | bytes 1048592 | tf_op jit(solution)/shard_map/all_gather | solution.py:113
  128.6 6.0 fusion.45
  135.9 192.4 %reduce-scatter.7.cloned.1.call-done = f32[32,512]{1,0:T(8,128)} async-done(((f32[32,8192]{1,0:T(8,128)}), f32[32,512]{1,0:T(8,128)}) %reduce-scatter.7.cloned.1.call-update) | async-done | bytes 65552 | tf_op jit(solution)/shard_map/reduce_scatter | solution.py:119
  328.3 66.4 %reduce-scatter.5.cloned.1.call-done = f32[32,512]{1,0:T(8,128)} async-done(((f32[32,8192]{1,0:T(8,128)}), f32[32,512]{1,0:T(8,128)}) %reduce-scatter.5.cloned.1.call-update) | async-done | bytes 65552 | tf_op jit(solution)/shard_map/reduce_scatter | solution.py:117
  395.7 78.8 %all-reduce.1 = (f32[16,16]{0,1:T(8,128)S(1)}, f32[16,16]{1,0:T(8,128)S(1)}) all-reduce(f32[16,16]{0,1:T(8,128)S(1)} %convolution_bitcast_fusion.1, f32[16,16]{1,0:T(8,128)S(1)} %fusion.72), channel_id=1, replica_groups=mesh['row'=16,'col'=16] {'row','col'}, use_global_device_ids=true, to_apply=%region_11.12 | all-reduce | flops 512 | bytes 4096 | tf_op jit(solution)/shard_map/psum | solution.py:122
  474.5 37.0 %while.135 = (s32[]{:T(128)}, f32[16,16]{1,0:T(8,128)S(1)}, f32[16,16]{1,0:T(8,128)S(1)}, s32[]{:T(128)}, s32[]{:T(128)}) while((s32[]{:T(128)}, f32[16,16]{1,0:T(8,128)S(1)}, f32[16,16]{1,0:T(8,128)S(1)}, s32[]{:T(128)}, s32[]{:T(128)}) %tuple.302), condition=%wide.region_10.11_spmd.clone.clone, body=%wide.region_4.10_spmd.clone.clone.sunk | while | flops 2978 | bytes 6069 | solution.py:28
  511.6 24.3 %while.129 = (s32[]{:T(128)}, f32[16,16]{1,0:T(8,128)S(1)}, f32[16,16]{1,0:T(8,128)S(1)}, f32[16,16]{1,0:T(8,128)S(1)}, s32[]{:T(128)}, /*index=5*/s32[]{:T(128)}) while((s32[]{:T(128)}, f32[16,16]{1,0:T(8,128)S(1)}, f32[16,16]{1,0:T(8,128)S(1)}, f32[16,16]{1,0:T(8,128)S(1)}, s32[]{:T(128)}, /*index=5*/s32[]{:T(128)}) %tuple.305), condition=%wide.region_17.18_spmd.clone, body=%wide.region_12.17_spmd.clone.sunk | while | flops 2626 | bytes 5984 | solution.py:43
  535.9 24.8 %while.130 = (s32[]{:T(128)}, f32[16,16]{1,0:T(8,128)S(1)}, f32[16,16]{1,0:T(8,128)S(1)}, f32[16,16]{1,0:T(8,128)S(1)}, s32[]{:T(128)}, /*index=5*/s32[]{:T(128)}, s32[]{:T(128)}) while((s32[]{:T(128)}, f32[16,16]{1,0:T(8,128)S(1)}, f32[16,16]{1,0:T(8,128)S(1)}, f32[16,16]{1,0:T(8,128)S(1)}, s32[]{:T(128)}, ...), condition=%wide.region_23.24_spmd.clone, body=%wide.region_18.23_spmd.clone.sunk | while | flops 2627 | bytes 6004 | solution.py:59
  560.9 19.6 %all_gather.15 = f32[16,8192]{1,0:T(8,128)S(1)} all-gather(f32[16,512]{1,0:T(8,128)S(1)} %convolution_subtract_fusion), channel_id=1, replica_groups=mesh['row'=16,'col'=16] {'row'}, dimensions={1}, use_global_device_ids=true | all-gather | bytes 557056 | tf_op jit(solution)/shard_map/all_gather | solution.py:132
  584.5 5.2 scatter_fusion.1
  590.6 34.6 %all_gather.14 = f32[16,8192]{1,0:T(8,128)S(1)} all-gather(f32[16,512]{1,0:T(8,128)S(1)} %convolution_subtract_fusion), channel_id=1, replica_groups=mesh['row'=16,'col'=16] {'col'}, dimensions={1}, use_global_device_ids=true | all-gather | bytes 557056 | tf_op jit(solution)/shard_map/all_gather | solution.py:131
  626.0 5.2 fusion.49
  632.8 145.4 %reduce-scatter.11.cloned.1.call-done = f32[16,512]{1,0:T(8,128)} async-done(((f32[16,8192]{1,0:T(8,128)}), f32[16,512]{1,0:T(8,128)}) %reduce-scatter.11.cloned.1.call-update) | async-done | bytes 32784 | tf_op jit(solution)/shard_map/reduce_scatter | solution.py:139
  778.1 65.7 %reduce-scatter.9.cloned.1.call-done = f32[16,512]{1,0:T(8,128)} async-done(((f32[16,8192]{1,0:T(8,128)}), f32[16,512]{1,0:T(8,128)}) %reduce-scatter.9.cloned.1.call-update) | async-done | bytes 32784 | tf_op jit(solution)/shard_map/reduce_scatter | solution.py:137
  844.8 79.4 %all-reduce = (f32[48,48]{0,1:T(8,128)S(1)}, f32[48,48]{1,0:T(8,128)S(1)}) all-reduce(f32[48,48]{0,1:T(8,128)S(1)} %pad_maximum_fusion.1, f32[48,48]{1,0:T(8,128)S(1)} %fusion.70), channel_id=1, replica_groups=mesh['row'=16,'col'=16] {'row','col'}, use_global_device_ids=true, to_apply=%region_35.36 | all-reduce | flops 4608 | bytes 36864 | tf_op jit(solution)/shard_map/psum | solution.py:142
  924.3 111.3 %while.136 = (s32[]{:T(128)}, f32[48,48]{1,0:T(8,128)S(1)}, f32[48,48]{1,0:T(8,128)S(1)}, s32[]{:T(128)}, s32[]{:T(128)}) while((s32[]{:T(128)}, f32[48,48]{1,0:T(8,128)S(1)}, f32[48,48]{1,0:T(8,128)S(1)}, s32[]{:T(128)}, s32[]{:T(128)}) %tuple.311), condition=%wide.region_31.32_spmd.clone.clone, body=%wide.region_25.31_spmd.clone.clone.sunk | while | flops 25826 | bytes 48693 | solution.py:28
  1035.6 79.4 %while.131 = (s32[]{:T(128)}, f32[48,48]{1,0:T(8,128)S(1)}, f32[48,48]{1,0:T(8,128)S(1)}, f32[48,48]{1,0:T(8,128)S(1)}, s32[]{:T(128)}, /*index=5*/s32[]{:T(128)}) while((s32[]{:T(128)}, f32[48,48]{1,0:T(8,128)S(1)}, f32[48,48]{1,0:T(8,128)S(1)}, f32[48,48]{1,0:T(8,128)S(1)}, s32[]{:T(128)}, /*index=5*/s32[]{:T(128)}) %tuple.314), condition=%wide.region_41.42_spmd.clone, body=%wide.region_36.41_spmd.clone.sunk | while | flops 23234 | bytes 48480 | solution.py:43
  1115.1 79.4 %while.132 = (s32[]{:T(128)}, f32[48,48]{1,0:T(8,128)S(1)}, f32[48,48]{1,0:T(8,128)S(1)}, f32[48,48]{1,0:T(8,128)S(1)}, s32[]{:T(128)}, /*index=5*/s32[]{:T(128)}) while((s32[]{:T(128)}, f32[48,48]{1,0:T(8,128)S(1)}, f32[48,48]{1,0:T(8,128)S(1)}, f32[48,48]{1,0:T(8,128)S(1)}, s32[]{:T(128)}, /*index=5*/s32[]{:T(128)}) %tuple.344), condition=%wide.region_47.48_spmd.clone, body=%wide.region_42.47_spmd.clone.sunk | while | flops 23234 | bytes 48480 | solution.py:43
  1194.8 81.8 %while.133 = (s32[]{:T(128)}, f32[48,16]{0,1:T(8,128)S(1)}, f32[48,16]{0,1:T(8,128)S(1)}, f32[48,48]{1,0:T(8,128)S(1)}, s32[]{:T(128)}, /*index=5*/s32[]{:T(128)}, s32[]{:T(128)}) while((s32[]{:T(128)}, f32[48,16]{0,1:T(8,128)S(1)}, f32[48,16]{0,1:T(8,128)S(1)}, f32[48,48]{1,0:T(8,128)S(1)}, s32[]{:T(128)}, ...), condition=%wide.region_53.54_spmd.clone, body=%wide.region_48.53_spmd.clone.sunk | while | flops 10947 | bytes 23348 | solution.py:59
  1276.8 73.6 %psum.39 = f32[16,16]{1,0:T(8,128)S(1)} all-reduce(f32[16,16]{1,0:T(8,128)S(1)} %fusion.73), channel_id=1, replica_groups=mesh['row'=16,'col'=16] {'row','col'}, use_global_device_ids=true, to_apply=%region_54.55 | all-reduce | flops 256 | bytes 2048 | tf_op jit(solution)/shard_map/psum | solution.py:152
  1350.5 37.0 %while.137 = (s32[]{:T(128)}, f32[16,16]{1,0:T(8,128)S(1)}, f32[16,16]{1,0:T(8,128)S(1)}, s32[]{:T(128)}, s32[]{:T(128)}) while((s32[]{:T(128)}, f32[16,16]{1,0:T(8,128)S(1)}, f32[16,16]{1,0:T(8,128)S(1)}, s32[]{:T(128)}, s32[]{:T(128)}) %tuple.323), condition=%wide.region_61.62_spmd.clone.clone, body=%wide.region_55.61_spmd.clone.clone.sunk | while | flops 2978 | bytes 6069 | solution.py:28
  1387.5 26.3 %while.134 = (s32[]{:T(128)}, f32[16,512]{1,0:T(8,128)S(1)}, f32[16,512]{1,0:T(8,128)S(1)}, f32[16,16]{1,0:T(8,128)S(1)}, s32[]{:T(128)}, /*index=5*/s32[]{:T(128)}) while((s32[]{:T(128)}, f32[16,512]{1,0:T(8,128)S(1)}, f32[16,512]{1,0:T(8,128)S(1)}, f32[16,16]{1,0:T(8,128)S(1)}, s32[]{:T(128)}, /*index=5*/s32[]{:T(128)}) %tuple.326), condition=%wide.region_67.68_spmd.clone, body=%wide.region_62.67_spmd.clone.sunk | while | flops 66114 | bytes 144928 | solution.py:43
  (1706 shorter events, 420.2 us)
Async XLA Ops:
  7.2 41.9 %all-gather.5.cloned.1.call-start = ((), (), s32[]{:S(2)}) async-start(), calls=%async_computation.6 | async-start | bytes 1114112 | tf_op jit(solution)/shard_map/all_gather | solution.py:114
  8.7 0.6 copy-start.4
  9.4 117.1 %all-gather.3.cloned.1.call-start = ((), (), s32[]{:S(2)}) async-start(), calls=%async_computation.4 | async-start | bytes 1114112 | tf_op jit(solution)/shard_map/all_gather | solution.py:113
  10.1 318.2 %reduce-scatter.7.cloned.1.call-start = ((), (), s32[]{:S(2)}) async-start(), calls=%async_computation.7 | async-start | bytes 1114112 | tf_op jit(solution)/shard_map/reduce_scatter | solution.py:119
  61.7 333.0 %reduce-scatter.5.cloned.1.call-start = ((), (), s32[]{:S(2)}) async-start(), calls=%async_computation.5 | async-start | bytes 1114112 | tf_op jit(solution)/shard_map/reduce_scatter | solution.py:117
  134.6 1.2 copy-start.1
  135.7 642.4 %reduce-scatter.11.cloned.1.call-start = ((), (), s32[]{:S(2)}) async-start(), calls=%async_computation.9 | async-start | bytes 557056 | tf_op jit(solution)/shard_map/reduce_scatter | solution.py:139
  560.9 715.6 %copy-start.2 = (f32[16,512]{1,0:T(8,128)}, f32[16,512]{1,0:T(8,128)S(1)}, u32[]{:S(2)}) copy-start(f32[16,512]{1,0:T(8,128)S(1)} %convolution_subtract_fusion) | copy-start | bytes 98308
  590.5 253.3 %reduce-scatter.9.cloned.1.call-start = ((), (), s32[]{:S(2)}) async-start(), calls=%async_computation.8 | async-start | bytes 557056 | tf_op jit(solution)/shard_map/reduce_scatter | solution.py:137
  626.0 6.1 copy-start.3
  1194.5 219.9 %copy-start = (f32[48,48]{1,0:T(8,128)}, f32[48,48]{1,0:T(8,128)S(1)}, u32[]{:S(2)}) copy-start(f32[48,48]{1,0:T(8,128)S(1)} %get-tuple-element.811) | copy-start | bytes 27652
Sparse Core Ops, SparseCore 0:
  9.8 39.1 all-gather.4
  51.6 74.7 all-gather.2
  130.3 198.0 reduce-scatter.6
  330.7 63.9 reduce-scatter.4
  590.6 187.4 reduce-scatter.10
  780.5 63.2 reduce-scatter.8
where the time goes:
time: 1430 us; the launch traced here: 1420 us
  waiting for transfers between devices  572 us (40%)
  other arithmetic  410 us (29%)
  blocking collectives  286 us (20%)
  loops' own time  107 us (7%)
  matrix products  21.8 us (2%)
  between operations  14.4 us (1%)
    reduce_scatter x1, waiting for transfers between devices, per_device(): lax.psum_scatter(backward, 'col', scatter_dimension=1, tiled=True)  192 us
    reduce_scatter x1, waiting for transfers between devices, per_device(): lax.psum_scatter(backward_r, 'col', scatter_dimension=1, tiled=True)  145 us
    another operation x3, loops' own time, cholesky_lower(): return lax.fori_loop(0, order_small, column_step, jnp.zeros_like(matrix))  105 us
    div x128, other arithmetic, row_step(): value = (right_row - jnp.sum(row_now[:, None] * solved, axis=0)) / pivot  87.9 us
    reduce_sum x128, other arithmetic, row_step(): pivot = jnp.sum(row_now * pick)  85.7 us
    psum x1, blocking collectives, per_device(): lax.psum((outer(basis, basis), gram_apply), ('row', 'col'))  79.4 us
    psum x1, blocking collectives, per_device(): lax.psum((outer(block_vecs, block_vecs), outer(block_vecs, image_x)), ('r...  78.8 us
    psum x1, blocking collectives, per_device(): gram_fresh = lax.psum(outer(fresh, fresh), ('row', 'col'))  73.6 us
  transfers between devices with their start and end apart: 6, of which 6 were waited for; matrix products, arithmetic and copies ran while one was open for 2% of the time, Pallas kernels for 0%

commit v1 on v0

--- a/solution.py
+++ b/solution.py
@@ -149,7 +149,9 @@
     )
     mixing = solve_upper_t(factor, target)
     fresh = jnp.dot(mixing.T, basis, precision=highest, preferred_element_type=jnp.float32)
-    gram_fresh = lax.psum(outer(fresh, fresh), ("row", "col"))
+    x = outer(fresh, fresh)
+    pieces = lax.all_gather(x, ("row", "col"))
+    gram_fresh = jnp.sum(pieces, axis=0)
     factor_fresh = cholesky_lower(gram_fresh)
     x_next = math.sqrt(order_total) * solve_lower(factor_fresh, fresh)
     return (x_next, reduced, resid)

time: 1430 us -> 1980 us (1.38)
  blocking collectives: 286 us -> 826 us
    all_gather x0 -> x1, blocking collectives: none -> 614 us  [per_device(): pieces = lax.all_gather(x, ('row', 'col'))]
    psum x1 -> x0, blocking collectives: 73.6 us -> none  [per_device(): gram_fresh = lax.psum(outer(fresh, fresh), ('row', 'col'))]
where the time goes in v1:
time: 1980 us; the launch traced here: 1960 us
  blocking collectives  826 us (42%)
  waiting for transfers between devices  572 us (29%)
  other arithmetic  410 us (21%)
  loops' own time  107 us (5%)
  matrix products  21.8 us (1%)
    all_gather x1, blocking collectives, per_device(): pieces = lax.all_gather(x, ('row', 'col'))  614 us
    reduce_scatter x1, waiting for transfers between devices, per_device(): lax.psum_scatter(backward, 'col', scatter_dimension=1, tiled=True)  192 us
    reduce_scatter x1, waiting for transfers between devices, per_device(): lax.psum_scatter(backward_r, 'col', scatter_dimension=1, tiled=True)  145 us
    another operation x3, loops' own time, cholesky_lower(): return lax.fori_loop(0, order_small, column_step, jnp.zeros_like(matrix))  105 us
    div x128, other arithmetic, row_step(): value = (right_row - jnp.sum(row_now[:, None] * solved, axis=0)) / pivot  87.9 us
    reduce_sum x128, other arithmetic, row_step(): pivot = jnp.sum(row_now * pick)  85.7 us
    psum x1, blocking collectives, per_device(): lax.psum((outer(basis, basis), gram_apply), ('row', 'col'))  79.4 us
    psum x1, blocking collectives, per_device(): lax.psum((outer(block_vecs, block_vecs), outer(block_vecs, image_x)), ('r...  78.8 us
  transfers between devices with their start and end apart: 6, of which 6 were waited for; matrix products, arithmetic and copies ran while one was open for 2% of the time, Pallas kernels for 0%

profile of v1, /device:TPU:1, one launch (start us, length us, event | category | flops | bytes accessed | tf_op | source)
XLA Modules:
  0.0 1962.0 jit_solution(1395994409619123963)
XLA Ops:
  11.9 37.2 %all-gather.6.cloned.1.call-done = f32[32,8192]{1,0:T(8,128)} async-done(((f32[32,512]{1,0:T(8,128)}), f32[32,8192]{1,0:T(8,128)}) %all-gather.6.cloned.1.call-update) | async-done | bytes 1048592 | tf_op jit(solution)/shard_map/all_gather | solution.py:114
  54.9 5.7 scatter_fusion
  62.0 64.4 %all-gather.4.cloned.1.call-done = f32[32,8192]{1,0:T(8,128)} async-done(((f32[32,512]{1,0:T(8,128)}), f32[32,8192]{1,0:T(8,128)}) %all-gather.4.cloned.1.call-update) | async-done | bytes 1048592 | tf_op jit(solution)/shard_map/all_gather | solution.py:113
  128.6 6.0 fusion.45
  135.9 192.4 %reduce-scatter.7.cloned.1.call-done = f32[32,512]{1,0:T(8,128)} async-done(((f32[32,8192]{1,0:T(8,128)}), f32[32,512]{1,0:T(8,128)}) %reduce-scatter.7.cloned.1.call-update) | async-done | bytes 65552 | tf_op jit(solution)/shard_map/reduce_scatter | solution.py:119
  328.3 66.4 %reduce-scatter.5.cloned.1.call-done = f32[32,512]{1,0:T(8,128)} async-done(((f32[32,8192]{1,0:T(8,128)}), f32[32,512]{1,0:T(8,128)}) %reduce-scatter.5.cloned.1.call-update) | async-done | bytes 65552 | tf_op jit(solution)/shard_map/reduce_scatter | solution.py:117
  395.7 78.8 %all-reduce.1 = (f32[16,16]{0,1:T(8,128)S(1)}, f32[16,16]{1,0:T(8,128)S(1)}) all-reduce(f32[16,16]{0,1:T(8,128)S(1)} %convolution_bitcast_fusion.1, f32[16,16]{1,0:T(8,128)S(1)} %fusion.72), channel_id=1, replica_groups=mesh['row'=16,'col'=16] {'row','col'}, use_global_device_ids=true, to_apply=%region_11.12 | all-reduce | flops 512 | bytes 4096 | tf_op jit(solution)/shard_map/psum | solution.py:122
  474.5 37.0 %while.135 = (s32[]{:T(128)}, f32[16,16]{1,0:T(8,128)S(1)}, f32[16,16]{1,0:T(8,128)S(1)}, s32[]{:T(128)}, s32[]{:T(128)}) while((s32[]{:T(128)}, f32[16,16]{1,0:T(8,128)S(1)}, f32[16,16]{1,0:T(8,128)S(1)}, s32[]{:T(128)}, s32[]{:T(128)}) %tuple.302), condition=%wide.region_10.11_spmd.clone.clone, body=%wide.region_4.10_spmd.clone.clone.sunk | while | flops 2978 | bytes 6069 | solution.py:28
  511.6 24.3 %while.129 = (s32[]{:T(128)}, f32[16,16]{1,0:T(8,128)S(1)}, f32[16,16]{1,0:T(8,128)S(1)}, f32[16,16]{1,0:T(8,128)S(1)}, s32[]{:T(128)}, /*index=5*/s32[]{:T(128)}) while((s32[]{:T(128)}, f32[16,16]{1,0:T(8,128)S(1)}, f32[16,16]{1,0:T(8,128)S(1)}, f32[16,16]{1,0:T(8,128)S(1)}, s32[]{:T(128)}, /*index=5*/s32[]{:T(128)}) %tuple.305), condition=%wide.region_17.18_spmd.clone, body=%wide.region_12.17_spmd.clone.sunk | while | flops 2626 | bytes 5984 | solution.py:43
  535.9 24.8 %while.130 = (s32[]{:T(128)}, f32[16,16]{1,0:T(8,128)S(1)}, f32[16,16]{1,0:T(8,128)S(1)}, f32[16,16]{1,0:T(8,128)S(1)}, s32[]{:T(128)}, /*index=5*/s32[]{:T(128)}, s32[]{:T(128)}) while((s32[]{:T(128)}, f32[16,16]{1,0:T(8,128)S(1)}, f32[16,16]{1,0:T(8,128)S(1)}, f32[16,16]{1,0:T(8,128)S(1)}, s32[]{:T(128)}, ...), condition=%wide.region_23.24_spmd.clone, body=%wide.region_18.23_spmd.clone.sunk | while | flops 2627 | bytes 6004 | solution.py:59
  560.9 19.6 all_gather.21
  584.5 5.2 scatter_fusion.1
  590.6 34.6 %all_gather.20 = f32[16,8192]{1,0:T(8,128)S(1)} all-gather(f32[16,512]{1,0:T(8,128)S(1)} %convolution_subtract_fusion), channel_id=1, replica_groups=mesh['row'=16,'col'=16] {'col'}, dimensions={1}, use_global_device_ids=true | all-gather | bytes 557056 | tf_op jit(solution)/shard_map/all_gather | solution.py:131
  626.0 5.2 fusion.49
  632.8 145.4 %reduce-scatter.11.cloned.1.call-done = f32[16,512]{1,0:T(8,128)} async-done(((f32[16,8192]{1,0:T(8,128)}), f32[16,512]{1,0:T(8,128)}) %reduce-scatter.11.cloned.1.call-update) | async-done | bytes 32784 | tf_op jit(solution)/shard_map/reduce_scatter | solution.py:139
  778.2 65.7 %reduce-scatter.9.cloned.1.call-done = f32[16,512]{1,0:T(8,128)} async-done(((f32[16,8192]{1,0:T(8,128)}), f32[16,512]{1,0:T(8,128)}) %reduce-scatter.9.cloned.1.call-update) | async-done | bytes 32784 | tf_op jit(solution)/shard_map/reduce_scatter | solution.py:137
  844.9 79.4 %all-reduce = (f32[48,48]{0,1:T(8,128)S(1)}, f32[48,48]{1,0:T(8,128)S(1)}) all-reduce(f32[48,48]{0,1:T(8,128)S(1)} %pad_maximum_fusion.1, f32[48,48]{1,0:T(8,128)S(1)} %fusion.70), channel_id=1, replica_groups=mesh['row'=16,'col'=16] {'row','col'}, use_global_device_ids=true, to_apply=%region_35.36 | all-reduce | flops 4608 | bytes 36864 | tf_op jit(solution)/shard_map/psum | solution.py:142
  924.4 111.3 %while.136 = (s32[]{:T(128)}, f32[48,48]{1,0:T(8,128)S(1)}, f32[48,48]{1,0:T(8,128)S(1)}, s32[]{:T(128)}, s32[]{:T(128)}) while((s32[]{:T(128)}, f32[48,48]{1,0:T(8,128)S(1)}, f32[48,48]{1,0:T(8,128)S(1)}, s32[]{:T(128)}, s32[]{:T(128)}) %tuple.311), condition=%wide.region_31.32_spmd.clone.clone, body=%wide.region_25.31_spmd.clone.clone.sunk | while | flops 25826 | bytes 48693 | solution.py:28
  1035.6 79.4 %while.131 = (s32[]{:T(128)}, f32[48,48]{1,0:T(8,128)S(1)}, f32[48,48]{1,0:T(8,128)S(1)}, f32[48,48]{1,0:T(8,128)S(1)}, s32[]{:T(128)}, /*index=5*/s32[]{:T(128)}) while((s32[]{:T(128)}, f32[48,48]{1,0:T(8,128)S(1)}, f32[48,48]{1,0:T(8,128)S(1)}, f32[48,48]{1,0:T(8,128)S(1)}, s32[]{:T(128)}, /*index=5*/s32[]{:T(128)}) %tuple.314), condition=%wide.region_41.42_spmd.clone, body=%wide.region_36.41_spmd.clone.sunk | while | flops 23234 | bytes 48480 | solution.py:43
  1115.1 79.4 %while.132 = (s32[]{:T(128)}, f32[48,48]{1,0:T(8,128)S(1)}, f32[48,48]{1,0:T(8,128)S(1)}, f32[48,48]{1,0:T(8,128)S(1)}, s32[]{:T(128)}, /*index=5*/s32[]{:T(128)}) while((s32[]{:T(128)}, f32[48,48]{1,0:T(8,128)S(1)}, f32[48,48]{1,0:T(8,128)S(1)}, f32[48,48]{1,0:T(8,128)S(1)}, s32[]{:T(128)}, /*index=5*/s32[]{:T(128)}) %tuple.344), condition=%wide.region_47.48_spmd.clone, body=%wide.region_42.47_spmd.clone.sunk | while | flops 23234 | bytes 48480 | solution.py:43
  1194.8 81.8 %while.133 = (s32[]{:T(128)}, f32[48,16]{0,1:T(8,128)S(1)}, f32[48,16]{0,1:T(8,128)S(1)}, f32[48,48]{1,0:T(8,128)S(1)}, s32[]{:T(128)}, /*index=5*/s32[]{:T(128)}, s32[]{:T(128)}) while((s32[]{:T(128)}, f32[48,16]{0,1:T(8,128)S(1)}, f32[48,16]{0,1:T(8,128)S(1)}, f32[48,48]{1,0:T(8,128)S(1)}, s32[]{:T(128)}, ...), condition=%wide.region_53.54_spmd.clone, body=%wide.region_48.53_spmd.clone.sunk | while | flops 10947 | bytes 23348 | solution.py:59
  1276.9 614.0 %all-gather = f32[4096,16]{1,0:T(8,128)S(1)} all-gather(f32[16,16]{1,0:T(8,128)S(1)} %fusion.73), channel_id=2, replica_groups=mesh['row'=16,'col'=16] {'row','col'}, dimensions={0}, use_global_device_ids=true | all-gather | bytes 263168 | tf_op jit(solution)/shard_map/all_gather | solution.py:153
  1891.1 37.0 %while.137 = (s32[]{:T(128)}, f32[16,16]{1,0:T(8,128)S(1)}, f32[16,16]{1,0:T(8,128)S(1)}, s32[]{:T(128)}, s32[]{:T(128)}) while((s32[]{:T(128)}, f32[16,16]{1,0:T(8,128)S(1)}, f32[16,16]{1,0:T(8,128)S(1)}, s32[]{:T(128)}, s32[]{:T(128)}) %tuple.323), condition=%wide.region_61.62_spmd.clone.clone, body=%wide.region_55.61_spmd.clone.clone.sunk | while | flops 2978 | bytes 6069 | solution.py:28
  1928.2 26.3 %while.134 = (s32[]{:T(128)}, f32[16,512]{1,0:T(8,128)S(1)}, f32[16,512]{1,0:T(8,128)S(1)}, f32[16,16]{1,0:T(8,128)S(1)}, s32[]{:T(128)}, /*index=5*/s32[]{:T(128)}) while((s32[]{:T(128)}, f32[16,512]{1,0:T(8,128)S(1)}, f32[16,512]{1,0:T(8,128)S(1)}, f32[16,16]{1,0:T(8,128)S(1)}, s32[]{:T(128)}, /*index=5*/s32[]{:T(128)}) %tuple.326), condition=%wide.region_67.68_spmd.clone, body=%wide.region_62.67_spmd.clone.sunk | while | flops 66114 | bytes 144928 | solution.py:43
  (1707 shorter events, 420.4 us)
Async XLA Ops:
  7.2 41.9 %all-gather.6.cloned.1.call-start = ((), (), s32[]{:S(2)}) async-start(), calls=%async_computation.6 | async-start | bytes 1114112 | tf_op jit(solution)/shard_map/all_gather | solution.py:114
  8.7 0.6 copy-start.4
  9.4 117.1 %all-gather.4.cloned.1.call-start = ((), (), s32[]{:S(2)}) async-start(), calls=%async_computation.4 | async-start | bytes 1114112 | tf_op jit(solution)/shard_map/all_gather | solution.py:113
  10.1 318.2 %reduce-scatter.7.cloned.1.call-start = ((), (), s32[]{:S(2)}) async-start(), calls=%async_computation.7 | async-start | bytes 1114112 | tf_op jit(solution)/shard_map/reduce_scatter | solution.py:119
  61.7 333.0 %reduce-scatter.5.cloned.1.call-start = ((), (), s32[]{:S(2)}) async-start(), calls=%async_computation.5 | async-start | bytes 1114112 | tf_op jit(solution)/shard_map/reduce_scatter | solution.py:117
  134.6 1.2 copy-start.1
  135.7 642.5 %reduce-scatter.11.cloned.1.call-start = ((), (), s32[]{:S(2)}) async-start(), calls=%async_computation.9 | async-start | bytes 557056 | tf_op jit(solution)/shard_map/reduce_scatter | solution.py:139
  560.9 715.6 %copy-start.2 = (f32[16,512]{1,0:T(8,128)}, f32[16,512]{1,0:T(8,128)S(1)}, u32[]{:S(2)}) copy-start(f32[16,512]{1,0:T(8,128)S(1)} %convolution_subtract_fusion) | copy-start | bytes 98308
  590.5 253.3 %reduce-scatter.9.cloned.1.call-start = ((), (), s32[]{:S(2)}) async-start(), calls=%async_computation.8 | async-start | bytes 557056 | tf_op jit(solution)/shard_map/reduce_scatter | solution.py:137
  626.0 6.1 copy-start.3
  1194.6 696.6 %copy-start = (f32[48,48]{1,0:T(8,128)}, f32[48,48]{1,0:T(8,128)S(1)}, u32[]{:S(2)}) copy-start(f32[48,48]{1,0:T(8,128)S(1)} %get-tuple-element.811) | copy-start | bytes 27652
Sparse Core Ops, SparseCore 0:
  9.8 39.1 all-gather.5
  51.6 74.7 all-gather.3
  130.3 198.0 reduce-scatter.6
  330.7 63.9 reduce-scatter.4
  590.7 187.4 reduce-scatter.10
  780.5 63.2 reduce-scatter.8
